TPU v7x, 32 devices: a whole 2x2x4 slice. The times are simulated.
32 devices in a mesh: gx: 4 (over z), gy: 2 (over core), gz: 4 (over y, x).
Axes of the slice: x: 2, y: 2, z: 4, core: 2. Of those that a mesh axis runs over, the one named last changes fastest.
Arguments:
- tokens: bfloat16 [16384, 768], P(('gx', 'gy', 'gz')), may hold values from -6 to 6
- segment_ids: int32 [8, 2048], P(('gx', 'gy')), may hold values from 0 to 15, never falling along the last dimension, each value on 1 to 1024 neighbouring positions
- valid_mask: int32 [8, 2048], P(('gx', 'gy')), may hold values from 0 to 1, as said below
- cotangent: bfloat16 [16384, 768], P(('gx', 'gy', 'gz')), may hold values from -6 to 6
- teacher: bfloat16 [16384, 768], P(('gx', 'gy', 'gz')), may hold values from -6 to 6
- w_query: bfloat16 [768, 768], P('gy', 'gz'), may hold values from -0.21875 to 0.21875
- b_query: bfloat16 [768], P('gz'), may hold values from -3 to 3
- w_key: bfloat16 [768, 768], P('gy', 'gz'), may hold values from -0.21875 to 0.21875
- w_value: bfloat16 [768, 768], P('gy', 'gz'), may hold values from -0.21875 to 0.21875
- b_value: bfloat16 [768], P('gz'), may hold values from -0.5 to 0.5
- w_out: bfloat16 [768, 768], P('gz', 'gy'), may hold values from -1.75 to 1.75
- b_out: bfloat16 [768], replicated, may hold values from -1.1953125 to 1.1953125
- norm1_gain: bfloat16 [768], replicated, may hold values from 0.5 to 1.5
- norm1_bias: bfloat16 [768], replicated, may hold values from -1.1953125 to 1.1953125
- w_up: bfloat16 [768, 3072], P('gy', 'gz'), may hold values from -0.21875 to 0.21875
- b_up: bfloat16 [3072], P('gz'), may hold values from -3 to 3
- w_down: bfloat16 [3072, 768], P('gz', 'gy'), may hold values from -0.109375 to 0.109375
- b_down: bfloat16 [768], replicated, may hold values from -1.1953125 to 1.1953125
- norm2_gain: bfloat16 [768], replicated, may hold values from 0.5 to 1.5
- norm2_bias: bfloat16 [768], replicated, may hold values from -1.1953125 to 1.1953125
Outputs:
- output: bfloat16 [16384, 768], P(('gx', 'gy', 'gz'))
- mean_loss: float32 [], replicated
- d_tokens: bfloat16 [16384, 768], P(('gx', 'gy', 'gz'))
- d_w_query: float32 [768, 768], P('gy', 'gz')
- d_b_query: float32 [768], P('gz')
- d_w_key: float32 [768, 768], P('gy', 'gz')
- d_w_value: float32 [768, 768], P('gy', 'gz')
- d_b_value: float32 [768], P('gz')
- d_w_out: float32 [768, 768], P('gz', 'gy')
- d_b_out: float32 [768], replicated
- d_norm1_gain: float32 [768], replicated
- d_norm1_bias: float32 [768], replicated
- d_w_up: float32 [768, 3072], P('gy', 'gz')
- d_b_up: float32 [3072], P('gz')
- d_w_down: float32 [3072, 768], P('gz', 'gy')
- d_b_down: float32 [768], replicated
- d_norm2_gain: float32 [768], replicated
- d_norm2_bias: float32 [768], replicated
Inputs may be any that keep to these rules, and one draw needn't show every extreme that they name: `segment_ids`: within a sequence the ids never fall, and each id that occurs forms one run of 1 to 1024 positions. `valid_mask`: in each sequence the valid tokens are a leading run of 512 positions or more, padding after it.
All inputs are finite; a program needn't handle non-finite values.
Results may differ from a plain program's by a relative error of at most 0.02.
Values may be sent and summed in bfloat16 or wider, within the bound.
No kernel may reach another device: no remote copies, remote signals or barrier semaphores. Data moves between devices by JAX's collectives and lax.ppermute only.
A program may use at most 128 MiB of HBM per device.

v0:
```python
import math
import jax
import jax.numpy as jnp
from jax import lax
from jax.sharding import PartitionSpec as P

HEAD = 64
MASKED = -1e30
EPSILON = 1e-05


def gather_rows(tensor):
    return lax.all_gather(tensor, "gz", axis=0, tiled=True)


def sum_rows(term_fn, row_count):
    return lax.psum_scatter(
        term_fn(jnp.int32(0), lax.axis_size("gz") * row_count).astype(jnp.bfloat16),
        "gz",
        scatter_dimension=0,
        tiled=True,
    ).astype(jnp.float32)


def norm_forward(resid, gain, shift):
    average = jnp.mean(resid, -1, keepdims=True)
    centered = resid - average
    inv_std = lax.rsqrt(jnp.mean(centered * centered, -1, keepdims=True) + EPSILON)
    normed = centered * inv_std
    return (normed * gain + shift, normed, inv_std)


def norm_backward(upstream, normed, inv_std, gain):
    d_gain = jnp.sum(upstream * normed, 0)
    d_shift = jnp.sum(upstream, 0)
    scaled = upstream * gain
    d_resid = inv_std * (
        scaled
        - jnp.mean(scaled, -1, keepdims=True)
        - normed * jnp.mean(scaled * normed, -1, keepdims=True)
    )
    return (d_resid, d_gain, d_shift)


def gelu_parts(preact):
    normal_cdf = 0.5 * (1.0 + lax.erf(preact * (1.0 / math.sqrt(2.0))))
    slope = normal_cdf + preact * jnp.exp(-0.5 * preact * preact) * (1.0 / math.sqrt(2.0 * math.pi))
    return (preact * normal_cdf, slope)


def allowed_block(seg_row, valid_row, first_row, block_rows):
    query_pos = first_row + jnp.arange(block_rows, dtype=jnp.int32)
    key_pos = jnp.arange(seg_row.shape[0], dtype=jnp.int32)
    query_seg = lax.dynamic_slice_in_dim(seg_row, first_row, block_rows)
    return (query_seg[:, None] == seg_row[None, :]) & (
        (valid_row[None, :] == 1) | (query_pos[:, None] == key_pos[None, :])
    )


def attention_forward(queries, key_rows, value_rows, seg_row, valid_row, block_rows):
    length, col_width = queries.shape
    head_count = col_width // HEAD
    score_scale = HEAD ** (-0.5)

    def one_block(block_index):
        first_row = block_index * block_rows
        allowed = allowed_block(seg_row, valid_row, first_row, block_rows)
        query_block = lax.dynamic_slice_in_dim(queries, first_row, block_rows)
        outputs = []
        log_parts = []
        for head_index in range(head_count):
            columns = slice(head_index * HEAD, (head_index + 1) * HEAD)
            scores = (
                jnp.einsum(
                    "qd,kd->qk",
                    query_block[:, columns],
                    key_rows[:, columns],
                    preferred_element_type=jnp.float32,
                )
                * score_scale
            )
            scores = jnp.where(allowed, scores, MASKED)
            row_max = jnp.max(scores, -1, keepdims=True)
            weights = jnp.exp(scores - row_max)
            exp_total = jnp.sum(weights, -1, keepdims=True)
            probs_low = (weights / exp_total).astype(jnp.bfloat16)
            outputs.append(
                jnp.dot(probs_low, value_rows[:, columns], preferred_element_type=jnp.float32)
            )
            log_parts.append((row_max + jnp.log(exp_total))[:, 0])
        return (jnp.concatenate(outputs, 1), jnp.stack(log_parts, 1))

    outputs, log_sums = lax.map(one_block, jnp.arange(length // block_rows, dtype=jnp.int32))
    return (outputs.reshape(length, col_width), log_sums.reshape(length, head_count))


def attention_backward(
    queries, key_rows, value_rows, d_attended, log_sums, seg_row, valid_row, block_rows
):
    length, col_width = queries.shape
    head_count = col_width // HEAD
    score_scale = HEAD ** (-0.5)

    def one_block(carried, block_index):
        d_key_sum, d_value_sum = carried
        first_row = block_index * block_rows
        allowed = allowed_block(seg_row, valid_row, first_row, block_rows)
        query_block = lax.dynamic_slice_in_dim(queries, first_row, block_rows)
        grad_block = lax.dynamic_slice_in_dim(d_attended, first_row, block_rows)
        log_block = lax.dynamic_slice_in_dim(log_sums, first_row, block_rows)
        query_parts = []
        key_parts = []
        value_parts = []
        for head_index in range(head_count):
            columns = slice(head_index * HEAD, (head_index + 1) * HEAD)
            scores = (
                jnp.einsum(
                    "qd,kd->qk",
                    query_block[:, columns],
                    key_rows[:, columns],
                    preferred_element_type=jnp.float32,
                )
                * score_scale
            )
            scores = jnp.where(allowed, scores, MASKED)
            probs = jnp.exp(scores - log_block[:, head_index : head_index + 1])
            d_probs = jnp.einsum(
                "qd,kd->qk",
                grad_block[:, columns],
                value_rows[:, columns],
                preferred_element_type=jnp.float32,
            )
            d_scores = (probs * (d_probs - jnp.sum(probs * d_probs, -1, keepdims=True))).astype(
                jnp.bfloat16
            )
            query_parts.append(
                jnp.dot(d_scores, key_rows[:, columns], preferred_element_type=jnp.float32)
                * score_scale
            )
            key_parts.append(
                jnp.einsum(
                    "qk,qd->kd",
                    d_scores,
                    query_block[:, columns],
                    preferred_element_type=jnp.float32,
                )
                * score_scale
            )
            value_parts.append(
                jnp.einsum(
                    "qk,qd->kd",
                    probs.astype(jnp.bfloat16),
                    grad_block[:, columns],
                    preferred_element_type=jnp.float32,
                )
            )
        d_key_sum = d_key_sum + jnp.concatenate(key_parts, 1)
        d_value_sum = d_value_sum + jnp.concatenate(value_parts, 1)
        return ((d_key_sum, d_value_sum), jnp.concatenate(query_parts, 1))

    zero_rows = jnp.zeros((length, col_width), jnp.float32)
    (d_key_sum, d_value_sum), d_query_blocks = lax.scan(
        one_block, (zero_rows, zero_rows), jnp.arange(length // block_rows, dtype=jnp.int32)
    )
    return (d_query_blocks.reshape(length, col_width), d_key_sum, d_value_sum)


def shards(
    tokens,
    segment_ids,
    valid_mask,
    cotangent,
    teacher,
    w_query,
    b_query,
    w_key,
    w_value,
    b_value,
    w_out,
    b_out,
    norm1_gain,
    norm1_bias,
    w_up,
    b_up,
    w_down,
    b_down,
    norm2_gain,
    norm2_bias,
):
    row_count = tokens.shape[0]
    group_rows = row_count * lax.axis_size("gz")
    block_rows = min(512, group_rows)
    own_first = lax.axis_index("gz") * row_count
    seg_row = segment_ids[0]
    valid_row = valid_mask[0]
    own_valid = lax.dynamic_slice_in_dim(valid_row, own_first, row_count).astype(jnp.float32)[
        :, None
    ]
    query_cols, key_cols, value_cols, up_cols = (
        lax.all_gather(w_query, "gy", axis=0, tiled=True),
        lax.all_gather(w_key, "gy", axis=0, tiled=True),
        lax.all_gather(w_value, "gy", axis=0, tiled=True),
        lax.all_gather(w_up, "gy", axis=0, tiled=True),
    )
    out_rows, down_rows = (
        lax.all_gather(w_out, "gy", axis=1, tiled=True),
        lax.all_gather(w_down, "gy", axis=1, tiled=True),
    )
    col_width = query_cols.shape[1]
    qkv_weight = jnp.concatenate([query_cols, key_cols, value_cols], 1)
    qkv_bias = jnp.concatenate(
        [
            b_query.astype(jnp.float32),
            jnp.zeros((col_width,), jnp.float32),
            b_value.astype(jnp.float32),
        ]
    )
    tokens_all = gather_rows(tokens)
    projected = (
        jnp.dot(tokens_all, qkv_weight, preferred_element_type=jnp.float32) + qkv_bias
    ).astype(jnp.bfloat16)
    queries = projected[:, :col_width]
    key_rows = projected[:, col_width : 2 * col_width]
    value_rows = projected[:, 2 * col_width :]
    attended, log_sums = attention_forward(
        queries, key_rows, value_rows, seg_row, valid_row, block_rows
    )
    attended = attended.astype(jnp.bfloat16)

    def out_term(first_row, span_rows):
        return jnp.dot(
            lax.dynamic_slice_in_dim(attended, first_row, span_rows),
            out_rows,
            preferred_element_type=jnp.float32,
        )

    mixed_rows = sum_rows(out_term, row_count) + b_out.astype(jnp.float32)
    resid1 = tokens.astype(jnp.float32) + mixed_rows
    hidden, normed1, inv_std1 = norm_forward(
        resid1, norm1_gain.astype(jnp.float32), norm1_bias.astype(jnp.float32)
    )
    hidden_low = hidden.astype(jnp.bfloat16)
    hidden_all = gather_rows(hidden_low)
    preact = jnp.dot(hidden_all, up_cols, preferred_element_type=jnp.float32) + b_up.astype(
        jnp.float32
    )
    activated, slope = gelu_parts(preact)
    activated = activated.astype(jnp.bfloat16)

    def down_term(first_row, span_rows):
        return jnp.dot(
            lax.dynamic_slice_in_dim(activated, first_row, span_rows),
            down_rows,
            preferred_element_type=jnp.float32,
        )

    branch = sum_rows(down_term, row_count)
    resid2 = hidden + (branch + b_down.astype(jnp.float32))
    norm2_gain_f = norm2_gain.astype(jnp.float32)
    output_full, normed2, inv_std2 = norm_forward(
        resid2, norm2_gain_f, norm2_bias.astype(jnp.float32)
    )
    mismatch = output_full - teacher.astype(jnp.float32)
    error_part = jnp.sum(own_valid * mismatch * mismatch)
    count_part = jnp.sum(own_valid)
    d_output = cotangent.astype(jnp.float32) + own_valid * mismatch
    d_resid2, d_norm2_gain, d_norm2_bias = norm_backward(d_output, normed2, inv_std2, norm2_gain_f)
    d_branch = d_resid2.astype(jnp.bfloat16)
    d_b_down = jnp.sum(d_branch, 0, dtype=jnp.float32)
    d_branch_all = gather_rows(d_branch)
    d_act = jnp.einsum("lm,fm->lf", d_branch_all, down_rows, preferred_element_type=jnp.float32)
    d_down = jnp.einsum("lf,lm->fm", activated, d_branch_all, preferred_element_type=jnp.float32)
    d_pre = (d_act * slope).astype(jnp.bfloat16)
    d_bias_up = jnp.sum(d_pre, 0, dtype=jnp.float32)
    d_up = jnp.einsum("lm,lf->mf", hidden_all, d_pre, preferred_element_type=jnp.float32)

    def back_term(first_row, span_rows):
        return jnp.einsum(
            "lf,mf->lm",
            lax.dynamic_slice_in_dim(d_pre, first_row, span_rows),
            up_cols,
            preferred_element_type=jnp.float32,
        )

    d_hidden = d_resid2 + sum_rows(back_term, row_count)
    d_resid1, d_norm1_gain, d_norm1_bias = norm_backward(
        d_hidden, normed1, inv_std1, norm1_gain.astype(jnp.float32)
    )
    d_mixed = d_resid1.astype(jnp.bfloat16)
    d_b_out = jnp.sum(d_mixed, 0, dtype=jnp.float32)
    d_mixed_all = gather_rows(d_mixed)
    d_attended = jnp.einsum(
        "lm,cm->lc", d_mixed_all, out_rows, preferred_element_type=jnp.float32
    ).astype(jnp.bfloat16)
    d_out_w = jnp.einsum("lc,lm->cm", attended, d_mixed_all, preferred_element_type=jnp.float32)
    d_query_rows, d_key_rows, d_value_rows = attention_backward(
        queries, key_rows, value_rows, d_attended, log_sums, seg_row, valid_row, block_rows
    )
    d_projected = jnp.concatenate([d_query_rows, d_key_rows, d_value_rows], 1).astype(jnp.bfloat16)
    d_qkv_w = jnp.einsum("lm,lc->mc", tokens_all, d_projected, preferred_element_type=jnp.float32)
    d_bias_qkv = jnp.sum(d_projected, 0, dtype=jnp.float32)

    def input_term(first_row, span_rows):
        return jnp.einsum(
            "lc,mc->lm",
            lax.dynamic_slice_in_dim(d_projected, first_row, span_rows),
            qkv_weight,
            preferred_element_type=jnp.float32,
        )

    d_tokens = d_resid1 + sum_rows(input_term, row_count)
    grad_query, grad_key, grad_value, grad_up = (
        lax.psum_scatter(
            d_qkv_w[:, :col_width].astype(jnp.bfloat16), "gy", scatter_dimension=0, tiled=True
        ).astype(jnp.float32),
        lax.psum_scatter(
            d_qkv_w[:, col_width : 2 * col_width].astype(jnp.bfloat16),
            "gy",
            scatter_dimension=0,
            tiled=True,
        ).astype(jnp.float32),
        lax.psum_scatter(
            d_qkv_w[:, 2 * col_width :].astype(jnp.bfloat16), "gy", scatter_dimension=0, tiled=True
        ).astype(jnp.float32),
        lax.psum_scatter(d_up.astype(jnp.bfloat16), "gy", scatter_dimension=0, tiled=True).astype(
            jnp.float32
        ),
    )
    grad_out, grad_down = (
        lax.psum_scatter(
            d_out_w.astype(jnp.bfloat16), "gy", scatter_dimension=1, tiled=True
        ).astype(jnp.float32),
        lax.psum_scatter(d_down.astype(jnp.bfloat16), "gy", scatter_dimension=1, tiled=True).astype(
            jnp.float32
        ),
    )
    grad_query, grad_key, grad_value, grad_up, grad_out, grad_down = (
        lax.psum(grad_query.astype(jnp.bfloat16), "gx").astype(jnp.float32),
        lax.psum(grad_key.astype(jnp.bfloat16), "gx").astype(jnp.float32),
        lax.psum(grad_value.astype(jnp.bfloat16), "gx").astype(jnp.float32),
        lax.psum(grad_up.astype(jnp.bfloat16), "gx").astype(jnp.float32),
        lax.psum(grad_out.astype(jnp.bfloat16), "gx").astype(jnp.float32),
        lax.psum(grad_down.astype(jnp.bfloat16), "gx").astype(jnp.float32),
    )
    grad_b_query, grad_b_value, grad_b_up = lax.psum(
        (d_bias_qkv[:col_width], d_bias_qkv[2 * col_width :], d_bias_up), ("gx", "gy")
    )
    (
        grad_gain1,
        grad_shift1,
        grad_gain2,
        grad_shift2,
        grad_b_out,
        grad_b_down,
        error_sum,
        count_sum,
    ) = lax.psum(
        (
            d_norm1_gain,
            d_norm1_bias,
            d_norm2_gain,
            d_norm2_bias,
            d_b_out,
            d_b_down,
            error_part,
            count_part,
        ),
        ("gx", "gy", "gz"),
    )
    mean_loss = error_sum / (count_sum * tokens.shape[1])
    return (
        output_full.astype(jnp.bfloat16),
        mean_loss,
        d_tokens.astype(jnp.bfloat16),
        grad_query,
        grad_b_query,
        grad_key,
        grad_value,
        grad_b_value,
        grad_out,
        grad_b_out,
        grad_gain1,
        grad_shift1,
        grad_up,
        grad_b_up,
        grad_down,
        grad_b_down,
        grad_gain2,
        grad_shift2,
    )


def solution(mesh):
    placed = (
        P(("gx", "gy", "gz"), None),
        P(("gx", "gy"), None),
        P(("gx", "gy"), None),
        P(("gx", "gy", "gz"), None),
        P(("gx", "gy", "gz"), None),
        P("gy", "gz"),
        P("gz"),
        P("gy", "gz"),
        P("gy", "gz"),
        P("gz"),
        P("gz", "gy"),
        P(),
        P(),
        P(),
        P("gy", "gz"),
        P("gz"),
        P("gz", "gy"),
        P(),
        P(),
        P(),
    )
    return jax.shard_map(
        shards,
        mesh=mesh,
        in_specs=placed,
        out_specs=(
            P(("gx", "gy", "gz"), None),
            P(),
            P(("gx", "gy", "gz"), None),
            P("gy", "gz"),
            P("gz"),
            P("gy", "gz"),
            P("gy", "gz"),
            P("gz"),
            P("gz", "gy"),
            P(),
            P(),
            P(),
            P("gy", "gz"),
            P("gz"),
            P("gz", "gy"),
            P(),
            P(),
            P(),
        ),
        check_vma=False,
    )
```

profile of v0, /device:TPU:0, one launch (start us, length us, event | category | flops | bytes accessed | tf_op | source)
XLA Modules:
  0.0 751.6 jit_solution(14504390201831847154)
XLA Ops:
  10.1 2.4 all_gather.34
  12.5 2.3 all_gather.30
  14.8 2.3 all_gather.31
  17.1 2.3 all_gather.32
  19.5 37.9 %all-gather.7.cloned.1.call-done = bf16[2048,768]{1,0:T(8,128)(2,1)} async-done(((bf16[512,768]{1,0:T(8,128)(2,1)}), bf16[2048,768]{1,0:T(8,128)(2,1)}) %all-gather.7.cloned.1.call-update) | async-done | bytes 3145744 | tf_op jit(solution)/shard_map/all_gather | solution.py:13
  57.4 3.9 fusion.63
  66.1 52.2 %while.27 = (s32[]{:T(128)}, bf16[4,512,192]{1,2,0:T(8,128)(2,1)}, f32[4,512,3]{1,2,0:T(4,128)S(1)}, s32[4]{0:T(128)S(1)}, s32[2048]{0:T(1024)S(1)}, /*index=5*/...) while((s32[]{:T(128)}, bf16[4,512,192]{1,2,0:T(8,128)(2,1)}, ...), condition=%wide.region_7.8_spmd, body=%wide.region_0.7_spmd.sunk | while | flops 843649024 | bytes 42000656 | solution.py:93
  67.4 1.9 fusion.158
  71.2 1.8 fusion.155
  80.5 1.9 fusion.158
  84.3 1.8 fusion.155
  93.5 1.9 fusion.158
  97.3 1.8 fusion.155
  100.9 1.8 fusion.161
  106.6 1.9 fusion.158
  110.4 1.8 fusion.155
  120.8 2.7 convolution_convert_fusion.3
  124.6 43.0 %reduce-scatter.21.cloned.1.call-done = bf16[512,768]{1,0:T(8,128)(2,1)} async-done(((bf16[2048,768]{1,0:T(8,128)(2,1)}), bf16[512,768]{1,0:T(8,128)(2,1)}) %reduce-scatter.21.cloned.1.call-update) | async-done | bytes 786448 | tf_op jit(solution)/shard_map/reduce_scatter | solution.py:17
  172.9 43.2 %all-gather.9.cloned.1.call-done = bf16[2048,768]{1,0:T(8,128)(2,1)} async-done(((bf16[512,768]{1,0:T(8,128)(2,1)}), bf16[2048,768]{1,0:T(8,128)(2,1)}) %all-gather.9.cloned.1.call-update) | async-done | bytes 3145744 | tf_op jit(solution)/shard_map/all_gather | solution.py:13
  216.1 7.0 multiply_convert_fusion.3
  223.0 3.6 all-gather.13.cloned.1.call-done
  226.6 6.5 convolution_convert_fusion.1
  234.4 43.8 %reduce-scatter.23.cloned.1.call-done = bf16[512,768]{1,0:T(8,128)(2,1)} async-done(((bf16[2048,768]{1,0:T(8,128)(2,1)}), bf16[512,768]{1,0:T(8,128)(2,1)}) %reduce-scatter.23.cloned.1.call-update) | async-done | bytes 786448 | tf_op jit(solution)/shard_map/reduce_scatter | solution.py:17
  278.2 2.3 fusion.69
  281.4 2.9 fusion.71
  284.3 3.0 convert_reduce_fusion.2
  287.4 44.1 %all-gather.15.cloned.1.call-done = bf16[2048,768]{1,0:T(8,128)(2,1)} async-done(((bf16[512,768]{1,0:T(8,128)(2,1)}), bf16[2048,768]{1,0:T(8,128)(2,1)}) %all-gather.15.cloned.1.call-update) | async-done | bytes 3145744 | tf_op jit(solution)/shard_map/all_gather | solution.py:13
  331.5 8.1 %convert_reduce_fusion = (f32[768]{0:T(1024)}, bf16[2048,768]{1,0:T(8,128)(2,1)S(1)}) fusion(f32[2048,768]{1,0:T(8,128)} %get-tuple-element.364, f32[768]{0:T(1024)S(1)} %convert_element_type.207, bf16[2048,768]{1,0:T(8,128)(2,1)} %all-gather.15.cloned.1.call-done, bf16[768,768]{1,0:T(8,128)(2,1)} %all-gather.13.cloned.1.call-done), kind=kOutput, calls=%fused_computation.103 | convolution fusion | flops 2436365568 | bytes 13768704 | tf_op jit(solution)/shard_map/lm,fm->lf/dot_general | solution.py:271
  341.2 4.0 convolution_convert_fusion
  345.3 43.9 %reduce-scatter.25.cloned.1.call-done = bf16[512,768]{1,0:T(8,128)(2,1)} async-done(((bf16[2048,768]{1,0:T(8,128)(2,1)}), bf16[512,768]{1,0:T(8,128)(2,1)}) %reduce-scatter.25.cloned.1.call-update) | async-done | bytes 786448 | tf_op jit(solution)/shard_map/reduce_scatter | solution.py:17
  389.2 3.5 multiply_reduce_fusion.4
  392.8 2.8 convert_reduce_fusion.3
  395.6 5.5 convolution_convert_fusion.5
  402.7 37.0 %all-gather.17.cloned.1.call-done = bf16[2048,768]{1,0:T(8,128)(2,1)} async-done(((bf16[512,768]{1,0:T(8,128)(2,1)}), bf16[2048,768]{1,0:T(8,128)(2,1)}) %all-gather.17.cloned.1.call-update) | async-done | bytes 3145744 | tf_op jit(solution)/shard_map/all_gather | solution.py:13
  439.7 4.0 convolution_convert_fusion.4
  444.6 106.6 %while.28 = (s32[]{:T(128)}, f32[2048,192]{0,1:T(8,128)}, f32[2048,192]{0,1:T(8,128)}, bf16[4,512,192]{1,2,0:T(8,128)(2,1)}, s32[4]{0:T(128)S(1)}, /*index=5*/s3...) while((s32[]{:T(128)}, f32[2048,192]{0,1:T(8,128)}, ...), condition=%wide.region_27.28_spmd.clone, body=%wide.region_23.27_spmd.clone.sunk | while | flops 2058486784 | bytes 141845040 | solution.py:162
  451.2 2.4 multiply_reduce_fusion.14
  456.7 2.5 multiply_reduce_fusion.15
  462.5 2.4 multiply_reduce_fusion.16
  477.8 2.4 multiply_reduce_fusion.14
  483.2 2.5 multiply_reduce_fusion.15
  489.1 2.4 multiply_reduce_fusion.16
  504.3 2.4 multiply_reduce_fusion.14
  509.8 2.5 multiply_reduce_fusion.15
  515.6 2.4 multiply_reduce_fusion.16
  530.9 2.4 multiply_reduce_fusion.14
  536.4 2.5 multiply_reduce_fusion.15
  542.2 2.4 multiply_reduce_fusion.16
  551.3 2.1 copy.80
  553.4 2.7 convolution_convert_fusion.8
  557.0 2.5 convert.16
  560.6 4.4 fusion.67
  568.0 6.5 convolution_convert_fusion.6
  574.7 2.2 copy.74
  581.0 9.4 %reduce-scatter.33.cloned.1.call-done = bf16[384,192]{1,0:T(8,128)(2,1)} async-done(((bf16[768,192]{1,0:T(8,128)(2,1)}), bf16[384,192]{1,0:T(8,128)(2,1)}) %reduce-scatter.33.cloned.1.call-update) | async-done | bytes 147472
  592.2 9.5 %reduce-scatter.31.cloned.1.call-done = bf16[384,192]{1,0:T(8,128)(2,1)} async-done(((bf16[768,192]{1,0:T(8,128)(2,1)}), bf16[384,192]{1,0:T(8,128)(2,1)}) %reduce-scatter.31.cloned.1.call-update) | async-done | bytes 147472
  603.3 10.9 %reduce-scatter.29.cloned.1.call-done = bf16[384,768]{1,0:T(8,128)(2,1)} async-done(((bf16[768,768]{1,0:T(8,128)(2,1)}), bf16[384,768]{1,0:T(8,128)(2,1)}) %reduce-scatter.29.cloned.1.call-update) | async-done | bytes 589840 | tf_op jit(solution)/shard_map/reduce_scatter | solution.py:325
  614.3 5.2 convolution_convert_fusion.2
  620.3 43.8 %all-reduce = (f32[]{:T(128)}, f32[]{:T(128)}, f32[768]{0:T(1024)}, f32[768]{0:T(1024)}, f32[768]{0:T(1024)}, /*index=5*/f32[768]{0:T(1024)}, f32[768]{0:T(1024)}, f32[768]{0:T(1024)}) all-reduce(f32[]{:T(128)} %get-tuple-element.262, f32[]{:T(128)} %get-tuple-element.334, ...), channel_id=1, replica_groups=mesh['gx'=4,'gy'=2,'gz'=4] {'gx','gy','gz'}, use_global_device_ids=true, to_apply=%region_15.16 | all-reduce | flops 4610 | bytes 36880 | tf_op jit(solution)/shard_map/psum | solution.py:357
  665.7 16.3 %all-reduce.1 = (f32[192]{0:T(256)}, f32[192]{0:T(256)}, f32[768]{0:T(1024)}) all-reduce(f32[192]{0:T(256)S(1)} %get-tuple-element.362, f32[192]{0:T(256)S(1)} %get-tuple-element.361, f32[768]{0:T(1024)S(1)} %copy-done.33), channel_id=1, replica_groups=mesh['gx'=4,'gy'=2,'gz'=4] {'gx','gy'}, use_global_device_ids=true, to_apply=%region_32.33 | all-reduce | flops 1152 | bytes 9216 | tf_op jit(solution)/shard_map/psum | solution.py:345
  682.0 12.6 %all-reduce.5.cloned.1.call-done = (bf16[384,192]{0,1:T(8,128)(2,1)}, bf16[384,192]{0,1:T(8,128)(2,1)}, bf16[384,192]{0,1:T(8,128)(2,1)}, bf16[192,384]{1,0:T(8,...) async-done(((bf16[384,192]{0,1:T(8,128)(2,1)}, bf16[384,192]{0,1:T(8,128)(2,1)}, bf16[384,192]{0,1:T(8,128)(2,1)}, bf16[192,384]{1,0:T(8,128)(2,1)}, ...) | async-done | bytes 1769488 | tf_op jit(solution)/shard_map/psum | solution.py:338
  701.4 2.2 convert_element_type.236
  704.6 35.9 %reduce-scatter.27.cloned.1.call-done = bf16[512,768]{1,0:T(8,128)(2,1)} async-done(((bf16[2048,768]{1,0:T(8,128)(2,1)}), bf16[512,768]{1,0:T(8,128)(2,1)}) %reduce-scatter.27.cloned.1.call-update) | async-done | bytes 786448 | tf_op jit(solution)/shard_map/reduce_scatter | solution.py:17
  740.5 2.2 add_convert_fusion.1
  (361 shorter events, 151.0 us)
Async XLA Ops:
  8.0 49.4 %all-gather.7.cloned.1.call-start = ((), (), s32[]{:S(2)}) async-start(), calls=%async_computation.10 | async-start | bytes 3932160 | tf_op jit(solution)/shard_map/all_gather | solution.py:13
  8.8 158.9 %reduce-scatter.21.cloned.1.call-start = ((), (), s32[]{:S(2)}) async-start(), calls=%async_computation.11 | async-start | bytes 3932160 | tf_op jit(solution)/shard_map/reduce_scatter | solution.py:17
  12.5 107.3 %copy-start.22 = (bf16[192,768]{1,0:T(8,128)(2,1)}, bf16[192,768]{1,0:T(8,128)(2,1)S(1)}, u32[]{:S(2)}) copy-start(bf16[192,768]{1,0:T(8,128)(2,1)S(1)} %all_gather.34) | copy-start | bytes 884740
  19.5 37.9 %copy-start.25 = (bf16[768,576]{0,1:T(8,128)(2,1)}, bf16[768,576]{0,1:T(8,128)(2,1)S(1)}, u32[]{:S(2)}) copy-start(bf16[768,576]{0,1:T(8,128)(2,1)S(1)} %constant_dynamic-update-slice_fusion) | copy-start | bytes 2654212
  63.1 2.9 copy-start.23
  63.1 2.9 copy-start.26
  118.2 1.6 copy-start.12
  123.5 1.1 copy-start.35
  123.5 1.1 copy-start.36
  123.5 44.2 %copy-start = (bf16[512,768]{1,0:T(8,128)(2,1)S(1)}, bf16[512,768]{1,0:T(8,128)(2,1)}, u32[]{:S(2)}) copy-start(bf16[512,768]{1,0:T(8,128)(2,1)} %param.24) | copy-start | bytes 2359300
  123.5 49.3 %all-gather.11.cloned.1.call-start = ((), (), s32[]{:S(2)}) async-start(), calls=%async_computation.13 | async-start | bytes 1769472 | tf_op jit(solution)/shard_map/all_gather | solution.py:203
  124.1 91.9 %all-gather.9.cloned.1.call-start = ((), (), s32[]{:S(2)}) async-start(), calls=%async_computation.12 | async-start | bytes 3932160 | tf_op jit(solution)/shard_map/all_gather | solution.py:13
  167.7 3.1 copy-start.6
  169.2 3.6 copy-start.37
  172.2 54.4 %all-gather.13.cloned.1.call-start = ((), (), s32[]{:S(2)}) async-start(), calls=%async_computation.14 | async-start | bytes 1769472 | tf_op jit(solution)/shard_map/all_gather | solution.py:207
  172.8 105.5 %reduce-scatter.23.cloned.1.call-start = ((), (), s32[]{:S(2)}) async-start(), calls=%async_computation.15 | async-start | bytes 3932160 | tf_op jit(solution)/shard_map/reduce_scatter | solution.py:17
  233.1 98.4 %all-gather.15.cloned.1.call-start = ((), (), s32[]{:S(2)}) async-start(), calls=%async_computation.16 | async-start | bytes 3932160 | tf_op jit(solution)/shard_map/all_gather | solution.py:13
  278.2 2.3 copy-start.7
  278.2 2.3 copy-start.14
  278.2 3.2 copy-start.17
  278.2 3.2 copy-start.18
  287.4 101.8 %reduce-scatter.25.cloned.1.call-start = ((), (), s32[]{:S(2)}) async-start(), calls=%async_computation.17 | async-start | bytes 3932160 | tf_op jit(solution)/shard_map/reduce_scatter | solution.py:17
  331.5 9.7 %copy-start.41 = (bf16[768,768]{1,0:T(8,128)(2,1)S(1)}, bf16[768,768]{1,0:T(8,128)(2,1)}, u32[]{:S(2)}) copy-start(bf16[768,768]{1,0:T(8,128)(2,1)} %all-gather.11.cloned.1.call-done) | copy-start | bytes 3538948
  339.6 1.7 copy-start.42
  345.3 94.4 %all-gather.17.cloned.1.call-start = ((), (), s32[]{:S(2)}) async-start(), calls=%async_computation.18 | async-start | bytes 3932160 | tf_op jit(solution)/shard_map/all_gather | solution.py:13
  389.2 3.6 copy-start.8
  389.2 3.6 copy-start.9
  389.2 3.6 copy-start.21
  395.6 179.1 %reduce-scatter.39.cloned.1.call-start = ((), (), s32[]{:S(2)}) async-start(), calls=%async_computation.25 | async-start | bytes 1769472
  402.6 174.3 %reduce-scatter.37.cloned.1.call-start = ((), (), s32[]{:S(2)}) async-start(), calls=%async_computation.24 | async-start | bytes 589824
  444.6 108.7 %copy-start.11 = (bf16[4,24,8,512]{3,2,0,1:T(8,128)(2,1)S(1)}, bf16[4,24,8,512]{3,2,0,1:T(8,128)(2,1)}, u32[]{:S(2)}) copy-start(bf16[4,24,8,512]{3,2,0,1:T(8,128)(2,1)} %copy-done.10) | copy-start | bytes 2359300
  449.5 1.7 copy-start.13
  466.7 1.4 copy-start.1
  466.7 1.9 copy-start.4
  469.6 1.3 copy-start.2
  469.7 1.7 copy-start.5
  476.1 1.7 copy-start.13
  493.2 1.4 copy-start.1
  493.2 1.9 copy-start.4
  496.2 1.3 copy-start.2
  496.2 1.7 copy-start.5
  502.6 1.7 copy-start.13
  519.8 1.4 copy-start.1
  519.8 1.9 copy-start.4
  522.8 1.3 copy-start.2
  522.8 1.7 copy-start.5
  529.2 1.7 copy-start.13
  546.4 1.4 copy-start.1
  546.4 1.9 copy-start.4
  549.3 1.3 copy-start.2
  549.3 1.7 copy-start.5
  556.0 3.4 copy-start.3
  557.0 3.5 copy-start.16
  560.5 18.8 %reduce-scatter.35.cloned.1.call-start = ((), (), s32[]{:S(2)}) async-start(), calls=%async_computation.23 | async-start | bytes 589824
  565.9 24.5 %reduce-scatter.33.cloned.1.call-start = ((), (), s32[]{:S(2)}) async-start(), calls=%async_computation.22 | async-start | bytes 589824
  566.9 34.7 %reduce-scatter.31.cloned.1.call-start = ((), (), s32[]{:S(2)}) async-start(), calls=%async_computation.21 | async-start | bytes 589824
  568.0 46.2 %reduce-scatter.29.cloned.1.call-start = ((), (), s32[]{:S(2)}) async-start(), calls=%async_computation.20 | async-start | bytes 1769472 | tf_op jit(solution)/shard_map/reduce_scatter | solution.py:325
  574.6 39.7 %copy-start.19 = (bf16[2048,192]{0,1:T(8,128)(2,1)S(1)}, bf16[2048,192]{0,1:T(8,128)(2,1)}, u32[]{:S(2)}) copy-start(bf16[2048,192]{0,1:T(8,128)(2,1)} %convert.16) | copy-start | bytes 2359300
  574.6 39.7 %copy-start.20 = (bf16[2048,192]{0,1:T(8,128)(2,1)S(1)}, bf16[2048,192]{0,1:T(8,128)(2,1)}, u32[]{:S(2)}) copy-start(bf16[2048,192]{0,1:T(8,128)(2,1)} %convert.17) | copy-start | bytes 2359300
  574.6 120.0 %all-reduce.5.cloned.1.call-start = ((), (), s32[]{:S(2)}) async-start(), calls=%async_computation.26 | async-start | bytes 3538944 | tf_op jit(solution)/shard_map/psum | solution.py:338
  614.2 126.3 %reduce-scatter.27.cloned.1.call-start = ((), (), s32[]{:S(2)}) async-start(), calls=%async_computation.19 | async-start | bytes 3932160 | tf_op jit(solution)/shard_map/reduce_scatter | solution.py:17
  619.5 46.2 %copy-start.33 = (f32[768]{0:T(1024)S(1)}, f32[768]{0:T(1024)}, u32[]{:S(2)}) copy-start(f32[768]{0:T(1024)} %get-tuple-element.365) | copy-start | bytes 9220
  694.6 8.9 %copy-start.24 = (bf16[768,384]{1,0:T(8,128)(2,1)S(1)}, bf16[768,384]{1,0:T(8,128)(2,1)}, u32[]{:S(2)}) copy-start(bf16[768,384]{1,0:T(8,128)(2,1)} %get-tuple-element.327) | copy-start | bytes 1769476
  696.3 44.2 %copy-start.15 = (f32[512,768]{1,0:T(8,128)S(1)}, f32[512,768]{1,0:T(8,128)}, u32[]{:S(2)}) copy-start(f32[512,768]{1,0:T(8,128)} %get-tuple-element.333) | copy-start | bytes 4718596
  (11 other events, 8.4 us)
Sparse Core Ops, SparseCore 0:
  10.7 46.6 all-gather.6
  123.7 43.9 reduce-scatter.20
  287.5 43.9 all-gather.14
  395.7 43.9 all-gather.16
  614.3 80.2 all-reduce.4
  697.7 42.7 reduce-scatter.26
Sparse Core Ops, SparseCore 1:
  125.5 9.1 all-gather.10
  172.3 43.7 all-gather.8
  217.5 9.1 all-gather.12
  233.2 45.0 reduce-scatter.22
  345.4 43.8 reduce-scatter.24
  402.7 8.6 reduce-scatter.38
  560.6 7.7 reduce-scatter.36
  570.4 8.8 reduce-scatter.34
  581.5 8.8 reduce-scatter.32
  592.7 8.8 reduce-scatter.30
  604.4 9.7 reduce-scatter.28
where the time goes:
time: 756 us; the launch traced here: 752 us
  waiting for transfers between devices  377 us (50%)
  matrix products  177 us (23%)
  blocking collectives  69.3 us (9%)
  other arithmetic  62.3 us (8%)
  local copies, waits for them, and re-layouts  39.4 us (5%)
  between operations  19 us (3%)
    reduce_scatter x4, waiting for transfers between devices, sum_rows(): lax.psum_scatter(term_fn(jnp.int32(0), lax.axis_size('gz') * row_count).a...  167 us
    all_gather x4, waiting for transfers between devices, gather_rows(): return lax.all_gather(tensor, 'gz', axis=0, tiled=True)  162 us
    dot_general x24, matrix products, one_block(): jnp.einsum('qd,kd->qk', query_block[:, columns], key_rows[:, columns], pr...  50.6 us
    psum x1, blocking collectives, shards(): lax.psum((d_norm1_gain, d_norm1_bias, d_norm2_gain, d_norm2_bias, d_b_out...  43.8 us
    unnamed x22, waiting for transfers between devices  21.5 us
    dot_general x12, matrix products, one_block(): jnp.einsum('qd,kd->qk', grad_block[:, columns], value_rows[:, columns], p...  19.6 us
    unnamed x88, local copies, waits for them, and re-layouts  18.3 us
    psum x1, blocking collectives, shards(): lax.psum((d_bias_qkv[:col_width], d_bias_qkv[2 * col_width:], d_bias_up),...  16.3 us
  transfers between devices with their start and end apart: 17, of which 14 were waited for; matrix products, arithmetic and copies ran while one was open for 23% of the time, Pallas kernels for 0%

commit v1 on v0

--- a/solution.py
+++ b/solution.py
@@ -343,7 +343,7 @@
         lax.psum(grad_down.astype(jnp.bfloat16), "gx").astype(jnp.float32),
     )
     grad_b_query, grad_b_value, grad_b_up = lax.psum(
-        (d_bias_qkv[:col_width], d_bias_qkv[2 * col_width :], d_bias_up), ("gx", "gy")
+        lax.psum((d_bias_qkv[:col_width], d_bias_qkv[2 * col_width :], d_bias_up), "gx"), "gy"
     )
     (
         grad_gain1,

time: 756 us -> 756 us (level)
  no operation moved by 1% of the time
where the time goes in v1:
time: 756 us; the launch traced here: 752 us
  waiting for transfers between devices  379 us (50%)
  matrix products  177 us (23%)
  blocking collectives  67.8 us (9%)
  other arithmetic  62.3 us (8%)
  local copies, waits for them, and re-layouts  39.4 us (5%)
  between operations  19 us (3%)
    reduce_scatter x4, waiting for transfers between devices, sum_rows(): lax.psum_scatter(term_fn(jnp.int32(0), lax.axis_size('gz') * row_count).a...  167 us
    all_gather x4, waiting for transfers between devices, gather_rows(): return lax.all_gather(tensor, 'gz', axis=0, tiled=True)  162 us
    dot_general x24, matrix products, one_block(): jnp.einsum('qd,kd->qk', query_block[:, columns], key_rows[:, columns], pr...  50.6 us
    psum x1, blocking collectives, shards(): lax.psum((d_norm1_gain, d_norm1_bias, d_norm2_gain, d_norm2_bias, d_b_out...  43.8 us
    unnamed x22, waiting for transfers between devices  21.5 us
    dot_general x12, matrix products, one_block(): jnp.einsum('qd,kd->qk', grad_block[:, columns], value_rows[:, columns], p...  19.6 us
    unnamed x88, local copies, waits for them, and re-layouts  18.3 us
    dot_general x12, matrix products, one_block(): jnp.einsum('qk,qd->kd', probs.astype(jnp.bfloat16), grad_block[:, columns...  16.1 us
  transfers between devices with their start and end apart: 17, of which 14 were waited for; matrix products, arithmetic and copies ran while one was open for 23% of the time, Pallas kernels for 0%

profile of v1, /device:TPU:0, one launch (start us, length us, event | category | flops | bytes accessed | tf_op | source)
XLA Modules:
  0.0 751.5 jit_solution(8580143545361707921)
XLA Ops:
  10.1 2.4 all_gather.34
  12.5 2.3 all_gather.30
  14.8 2.3 all_gather.31
  17.1 2.3 all_gather.32
  19.5 37.9 %all-gather.7.cloned.1.call-done = bf16[2048,768]{1,0:T(8,128)(2,1)} async-done(((bf16[512,768]{1,0:T(8,128)(2,1)}), bf16[2048,768]{1,0:T(8,128)(2,1)}) %all-gather.7.cloned.1.call-update) | async-done | bytes 3145744 | tf_op jit(solution)/shard_map/all_gather | solution.py:13
  57.4 3.9 fusion.63
  66.1 52.2 %while.27 = (s32[]{:T(128)}, bf16[4,512,192]{1,2,0:T(8,128)(2,1)}, f32[4,512,3]{1,2,0:T(4,128)S(1)}, s32[4]{0:T(128)S(1)}, s32[2048]{0:T(1024)S(1)}, /*index=5*/...) while((s32[]{:T(128)}, bf16[4,512,192]{1,2,0:T(8,128)(2,1)}, ...), condition=%wide.region_7.8_spmd, body=%wide.region_0.7_spmd.sunk | while | flops 843649024 | bytes 42000656 | solution.py:93
  67.4 1.9 fusion.158
  71.2 1.8 fusion.155
  80.5 1.9 fusion.158
  84.3 1.8 fusion.155
  93.5 1.9 fusion.158
  97.3 1.8 fusion.155
  106.6 1.9 fusion.158
  110.4 1.8 fusion.155
  120.8 2.7 convolution_convert_fusion.3
  124.6 43.0 %reduce-scatter.21.cloned.1.call-done = bf16[512,768]{1,0:T(8,128)(2,1)} async-done(((bf16[2048,768]{1,0:T(8,128)(2,1)}), bf16[512,768]{1,0:T(8,128)(2,1)}) %reduce-scatter.21.cloned.1.call-update) | async-done | bytes 786448 | tf_op jit(solution)/shard_map/reduce_scatter | solution.py:17
  172.9 43.2 %all-gather.9.cloned.1.call-done = bf16[2048,768]{1,0:T(8,128)(2,1)} async-done(((bf16[512,768]{1,0:T(8,128)(2,1)}), bf16[2048,768]{1,0:T(8,128)(2,1)}) %all-gather.9.cloned.1.call-update) | async-done | bytes 3145744 | tf_op jit(solution)/shard_map/all_gather | solution.py:13
  216.1 7.0 multiply_convert_fusion.3
  223.0 3.6 all-gather.13.cloned.1.call-done
  226.6 6.5 convolution_convert_fusion.1
  234.4 43.8 %reduce-scatter.23.cloned.1.call-done = bf16[512,768]{1,0:T(8,128)(2,1)} async-done(((bf16[2048,768]{1,0:T(8,128)(2,1)}), bf16[512,768]{1,0:T(8,128)(2,1)}) %reduce-scatter.23.cloned.1.call-update) | async-done | bytes 786448 | tf_op jit(solution)/shard_map/reduce_scatter | solution.py:17
  278.2 2.3 fusion.69
  281.4 2.9 fusion.71
  284.3 3.0 convert_reduce_fusion.2
  287.4 44.1 %all-gather.15.cloned.1.call-done = bf16[2048,768]{1,0:T(8,128)(2,1)} async-done(((bf16[512,768]{1,0:T(8,128)(2,1)}), bf16[2048,768]{1,0:T(8,128)(2,1)}) %all-gather.15.cloned.1.call-update) | async-done | bytes 3145744 | tf_op jit(solution)/shard_map/all_gather | solution.py:13
  331.5 8.1 %convert_reduce_fusion = (f32[768]{0:T(1024)}, bf16[2048,768]{1,0:T(8,128)(2,1)S(1)}) fusion(f32[2048,768]{1,0:T(8,128)} %get-tuple-element.367, f32[768]{0:T(1024)S(1)} %convert_element_type.207, bf16[2048,768]{1,0:T(8,128)(2,1)} %all-gather.15.cloned.1.call-done, bf16[768,768]{1,0:T(8,128)(2,1)} %all-gather.13.cloned.1.call-done), kind=kOutput, calls=%fused_computation.103 | convolution fusion | flops 2436365568 | bytes 13768704 | tf_op jit(solution)/shard_map/lm,fm->lf/dot_general | solution.py:271
  341.2 4.0 convolution_convert_fusion
  345.3 43.9 %reduce-scatter.25.cloned.1.call-done = bf16[512,768]{1,0:T(8,128)(2,1)} async-done(((bf16[2048,768]{1,0:T(8,128)(2,1)}), bf16[512,768]{1,0:T(8,128)(2,1)}) %reduce-scatter.25.cloned.1.call-update) | async-done | bytes 786448 | tf_op jit(solution)/shard_map/reduce_scatter | solution.py:17
  389.2 3.5 multiply_reduce_fusion.4
  392.8 2.8 convert_reduce_fusion.3
  395.6 5.5 convolution_convert_fusion.5
  402.7 37.0 %all-gather.17.cloned.1.call-done = bf16[2048,768]{1,0:T(8,128)(2,1)} async-done(((bf16[512,768]{1,0:T(8,128)(2,1)}), bf16[2048,768]{1,0:T(8,128)(2,1)}) %all-gather.17.cloned.1.call-update) | async-done | bytes 3145744 | tf_op jit(solution)/shard_map/all_gather | solution.py:13
  439.7 4.0 convolution_convert_fusion.4
  444.6 106.6 %while.28 = (s32[]{:T(128)}, f32[2048,192]{0,1:T(8,128)}, f32[2048,192]{0,1:T(8,128)}, bf16[4,512,192]{1,2,0:T(8,128)(2,1)}, s32[4]{0:T(128)S(1)}, /*index=5*/s3...) while((s32[]{:T(128)}, f32[2048,192]{0,1:T(8,128)}, ...), condition=%wide.region_27.28_spmd.clone, body=%wide.region_23.27_spmd.clone.sunk | while | flops 2058486784 | bytes 141845040 | solution.py:162
  451.2 2.4 multiply_reduce_fusion.14
  456.7 2.5 multiply_reduce_fusion.15
  462.5 2.4 multiply_reduce_fusion.16
  477.8 2.4 multiply_reduce_fusion.14
  483.2 2.5 multiply_reduce_fusion.15
  489.1 2.4 multiply_reduce_fusion.16
  504.3 2.4 multiply_reduce_fusion.14
  509.8 2.5 multiply_reduce_fusion.15
  515.6 2.4 multiply_reduce_fusion.16
  530.9 2.4 multiply_reduce_fusion.14
  536.4 2.5 multiply_reduce_fusion.15
  542.2 2.4 multiply_reduce_fusion.16
  551.3 2.1 copy.80
  553.4 2.7 convolution_convert_fusion.8
  557.0 2.5 convert.16
  560.6 4.4 fusion.67
  568.0 6.5 convolution_convert_fusion.6
  574.7 2.2 copy.74
  581.0 9.4 %reduce-scatter.33.cloned.1.call-done = bf16[384,192]{1,0:T(8,128)(2,1)} async-done(((bf16[768,192]{1,0:T(8,128)(2,1)}), bf16[384,192]{1,0:T(8,128)(2,1)}) %reduce-scatter.33.cloned.1.call-update) | async-done | bytes 147472
  592.2 9.5 %reduce-scatter.31.cloned.1.call-done = bf16[384,192]{1,0:T(8,128)(2,1)} async-done(((bf16[768,192]{1,0:T(8,128)(2,1)}), bf16[384,192]{1,0:T(8,128)(2,1)}) %reduce-scatter.31.cloned.1.call-update) | async-done | bytes 147472
  603.3 10.9 %reduce-scatter.29.cloned.1.call-done = bf16[384,768]{1,0:T(8,128)(2,1)} async-done(((bf16[768,768]{1,0:T(8,128)(2,1)}), bf16[384,768]{1,0:T(8,128)(2,1)}) %reduce-scatter.29.cloned.1.call-update) | async-done | bytes 589840 | tf_op jit(solution)/shard_map/reduce_scatter | solution.py:325
  614.3 5.2 convolution_convert_fusion.2
  620.3 43.8 %all-reduce = (f32[]{:T(128)}, f32[]{:T(128)}, f32[768]{0:T(1024)}, f32[768]{0:T(1024)}, f32[768]{0:T(1024)}, /*index=5*/f32[768]{0:T(1024)}, f32[768]{0:T(1024)}, f32[768]{0:T(1024)}) all-reduce(f32[]{:T(128)} %get-tuple-element.262, f32[]{:T(128)} %get-tuple-element.337, ...), channel_id=1, replica_groups=mesh['gx'=4,'gy'=2,'gz'=4] {'gx','gy','gz'}, use_global_device_ids=true, to_apply=%region_15.16 | all-reduce | flops 4610 | bytes 36880 | tf_op jit(solution)/shard_map/psum | solution.py:357
  665.7 11.7 %all-reduce.1 = (f32[192]{0:T(256)S(1)}, f32[192]{0:T(256)S(1)}, f32[768]{0:T(1024)S(1)}) all-reduce(f32[192]{0:T(256)S(1)} %get-tuple-element.365, f32[192]{0:T(256)S(1)} %get-tuple-element.364, f32[768]{0:T(1024)S(1)} %copy-done.33), channel_id=1, replica_groups=mesh['gx'=4,'gy'=2,'gz'=4] {'gx'}, use_global_device_ids=true, to_apply=%region_32.33 | all-reduce | flops 1152 | bytes 9216 | tf_op jit(solution)/shard_map/psum | solution.py:346
  677.5 3.1 all-reduce.2
  680.6 13.9 %all-reduce.6.cloned.1.call-done = (bf16[384,192]{0,1:T(8,128)(2,1)}, bf16[384,192]{0,1:T(8,128)(2,1)}, bf16[384,192]{0,1:T(8,128)(2,1)}, bf16[192,384]{1,0:T(8,...) async-done(((bf16[384,192]{0,1:T(8,128)(2,1)}, bf16[384,192]{0,1:T(8,128)(2,1)}, bf16[384,192]{0,1:T(8,128)(2,1)}, bf16[192,384]{1,0:T(8,128)(2,1)}, ...) | async-done | bytes 1769488 | tf_op jit(solution)/shard_map/psum | solution.py:338
  701.2 2.2 convert_element_type.236
  704.5 36.0 %reduce-scatter.27.cloned.1.call-done = bf16[512,768]{1,0:T(8,128)(2,1)} async-done(((bf16[2048,768]{1,0:T(8,128)(2,1)}), bf16[512,768]{1,0:T(8,128)(2,1)}) %reduce-scatter.27.cloned.1.call-update) | async-done | bytes 786448 | tf_op jit(solution)/shard_map/reduce_scatter | solution.py:17
  740.4 2.2 add_convert_fusion.1
  (362 shorter events, 152.7 us)
Async XLA Ops:
  8.0 49.4 %all-gather.7.cloned.1.call-start = ((), (), s32[]{:S(2)}) async-start(), calls=%async_computation.10 | async-start | bytes 3932160 | tf_op jit(solution)/shard_map/all_gather | solution.py:13
  8.8 158.9 %reduce-scatter.21.cloned.1.call-start = ((), (), s32[]{:S(2)}) async-start(), calls=%async_computation.11 | async-start | bytes 3932160 | tf_op jit(solution)/shard_map/reduce_scatter | solution.py:17
  12.5 107.3 %copy-start.22 = (bf16[192,768]{1,0:T(8,128)(2,1)}, bf16[192,768]{1,0:T(8,128)(2,1)S(1)}, u32[]{:S(2)}) copy-start(bf16[192,768]{1,0:T(8,128)(2,1)S(1)} %all_gather.34) | copy-start | bytes 884740
  19.5 37.9 %copy-start.25 = (bf16[768,576]{0,1:T(8,128)(2,1)}, bf16[768,576]{0,1:T(8,128)(2,1)S(1)}, u32[]{:S(2)}) copy-start(bf16[768,576]{0,1:T(8,128)(2,1)S(1)} %constant_dynamic-update-slice_fusion) | copy-start | bytes 2654212
  63.1 2.9 copy-start.23
  63.1 2.9 copy-start.26
  118.2 1.6 copy-start.12
  123.5 1.1 copy-start.35
  123.5 1.1 copy-start.36
  123.5 44.2 %copy-start = (bf16[512,768]{1,0:T(8,128)(2,1)S(1)}, bf16[512,768]{1,0:T(8,128)(2,1)}, u32[]{:S(2)}) copy-start(bf16[512,768]{1,0:T(8,128)(2,1)} %param.24) | copy-start | bytes 2359300
  123.5 49.3 %all-gather.11.cloned.1.call-start = ((), (), s32[]{:S(2)}) async-start(), calls=%async_computation.13 | async-start | bytes 1769472 | tf_op jit(solution)/shard_map/all_gather | solution.py:203
  124.1 91.9 %all-gather.9.cloned.1.call-start = ((), (), s32[]{:S(2)}) async-start(), calls=%async_computation.12 | async-start | bytes 3932160 | tf_op jit(solution)/shard_map/all_gather | solution.py:13
  167.7 3.1 copy-start.6
  169.2 3.6 copy-start.37
  172.2 54.4 %all-gather.13.cloned.1.call-start = ((), (), s32[]{:S(2)}) async-start(), calls=%async_computation.14 | async-start | bytes 1769472 | tf_op jit(solution)/shard_map/all_gather | solution.py:207
  172.8 105.5 %reduce-scatter.23.cloned.1.call-start = ((), (), s32[]{:S(2)}) async-start(), calls=%async_computation.15 | async-start | bytes 3932160 | tf_op jit(solution)/shard_map/reduce_scatter | solution.py:17
  233.1 98.4 %all-gather.15.cloned.1.call-start = ((), (), s32[]{:S(2)}) async-start(), calls=%async_computation.16 | async-start | bytes 3932160 | tf_op jit(solution)/shard_map/all_gather | solution.py:13
  278.2 2.3 copy-start.7
  278.2 2.3 copy-start.14
  278.2 3.2 copy-start.17
  278.2 3.2 copy-start.18
  287.4 101.8 %reduce-scatter.25.cloned.1.call-start = ((), (), s32[]{:S(2)}) async-start(), calls=%async_computation.17 | async-start | bytes 3932160 | tf_op jit(solution)/shard_map/reduce_scatter | solution.py:17
  331.5 9.7 %copy-start.41 = (bf16[768,768]{1,0:T(8,128)(2,1)S(1)}, bf16[768,768]{1,0:T(8,128)(2,1)}, u32[]{:S(2)}) copy-start(bf16[768,768]{1,0:T(8,128)(2,1)} %all-gather.11.cloned.1.call-done) | copy-start | bytes 3538948
  339.6 1.7 copy-start.42
  345.3 94.4 %all-gather.17.cloned.1.call-start = ((), (), s32[]{:S(2)}) async-start(), calls=%async_computation.18 | async-start | bytes 3932160 | tf_op jit(solution)/shard_map/all_gather | solution.py:13
  389.2 3.6 copy-start.8
  389.2 3.6 copy-start.9
  389.2 3.6 copy-start.21
  395.6 179.1 %reduce-scatter.39.cloned.1.call-start = ((), (), s32[]{:S(2)}) async-start(), calls=%async_computation.25 | async-start | bytes 1769472
  402.6 174.3 %reduce-scatter.37.cloned.1.call-start = ((), (), s32[]{:S(2)}) async-start(), calls=%async_computation.24 | async-start | bytes 589824
  444.6 108.7 %copy-start.11 = (bf16[4,24,8,512]{3,2,0,1:T(8,128)(2,1)S(1)}, bf16[4,24,8,512]{3,2,0,1:T(8,128)(2,1)}, u32[]{:S(2)}) copy-start(bf16[4,24,8,512]{3,2,0,1:T(8,128)(2,1)} %copy-done.10) | copy-start | bytes 2359300
  449.5 1.7 copy-start.13
  466.7 1.4 copy-start.1
  466.7 1.9 copy-start.4
  469.6 1.3 copy-start.2
  469.7 1.7 copy-start.5
  476.1 1.7 copy-start.13
  493.2 1.4 copy-start.1
  493.2 1.9 copy-start.4
  496.2 1.3 copy-start.2
  496.2 1.7 copy-start.5
  502.6 1.7 copy-start.13
  519.8 1.4 copy-start.1
  519.8 1.9 copy-start.4
  522.8 1.3 copy-start.2
  522.8 1.7 copy-start.5
  529.2 1.7 copy-start.13
  546.4 1.4 copy-start.1
  546.4 1.9 copy-start.4
  549.3 1.3 copy-start.2
  549.3 1.7 copy-start.5
  556.0 3.4 copy-start.3
  557.0 3.5 copy-start.16
  560.5 18.8 %reduce-scatter.35.cloned.1.call-start = ((), (), s32[]{:S(2)}) async-start(), calls=%async_computation.23 | async-start | bytes 589824
  565.9 24.5 %reduce-scatter.33.cloned.1.call-start = ((), (), s32[]{:S(2)}) async-start(), calls=%async_computation.22 | async-start | bytes 589824
  566.9 34.7 %reduce-scatter.31.cloned.1.call-start = ((), (), s32[]{:S(2)}) async-start(), calls=%async_computation.21 | async-start | bytes 589824
  568.0 46.2 %reduce-scatter.29.cloned.1.call-start = ((), (), s32[]{:S(2)}) async-start(), calls=%async_computation.20 | async-start | bytes 1769472 | tf_op jit(solution)/shard_map/reduce_scatter | solution.py:325
  574.6 39.7 %copy-start.19 = (bf16[2048,192]{0,1:T(8,128)(2,1)S(1)}, bf16[2048,192]{0,1:T(8,128)(2,1)}, u32[]{:S(2)}) copy-start(bf16[2048,192]{0,1:T(8,128)(2,1)} %convert.16) | copy-start | bytes 2359300
  574.6 39.7 %copy-start.20 = (bf16[2048,192]{0,1:T(8,128)(2,1)S(1)}, bf16[2048,192]{0,1:T(8,128)(2,1)}, u32[]{:S(2)}) copy-start(bf16[2048,192]{0,1:T(8,128)(2,1)} %convert.17) | copy-start | bytes 2359300
  574.6 119.8 %all-reduce.6.cloned.1.call-start = ((), (), s32[]{:S(2)}) async-start(), calls=%async_computation.26 | async-start | bytes 3538944 | tf_op jit(solution)/shard_map/psum | solution.py:338
  614.2 126.2 %reduce-scatter.27.cloned.1.call-start = ((), (), s32[]{:S(2)}) async-start(), calls=%async_computation.19 | async-start | bytes 3932160 | tf_op jit(solution)/shard_map/reduce_scatter | solution.py:17
  619.5 46.2 %copy-start.33 = (f32[768]{0:T(1024)S(1)}, f32[768]{0:T(1024)}, u32[]{:S(2)}) copy-start(f32[768]{0:T(1024)} %get-tuple-element.368) | copy-start | bytes 9220
  694.4 8.9 %copy-start.24 = (bf16[768,384]{1,0:T(8,128)(2,1)S(1)}, bf16[768,384]{1,0:T(8,128)(2,1)}, u32[]{:S(2)}) copy-start(bf16[768,384]{1,0:T(8,128)(2,1)} %get-tuple-element.330) | copy-start | bytes 1769476
  696.2 44.3 %copy-start.15 = (f32[512,768]{1,0:T(8,128)S(1)}, f32[512,768]{1,0:T(8,128)}, u32[]{:S(2)}) copy-start(f32[512,768]{1,0:T(8,128)} %get-tuple-element.336) | copy-start | bytes 4718596
  (11 other events, 8.4 us)
Sparse Core Ops, SparseCore 0:
  10.7 46.6 all-gather.6
  123.7 43.9 reduce-scatter.20
  287.5 43.9 all-gather.14
  395.7 43.9 all-gather.16
  614.3 80.0 all-reduce.5
  697.6 42.8 reduce-scatter.26
Sparse Core Ops, SparseCore 1:
  125.5 9.1 all-gather.10
  172.3 43.7 all-gather.8
  217.5 9.1 all-gather.12
  233.2 45.0 reduce-scatter.22
  345.4 43.8 reduce-scatter.24
  402.7 8.6 reduce-scatter.38
  560.6 7.7 reduce-scatter.36
  570.4 8.8 reduce-scatter.34
  581.5 8.8 reduce-scatter.32
  592.7 8.8 reduce-scatter.30
  604.4 9.7 reduce-scatter.28
